TPU v7x, 256 devices: a whole 4x4x8 slice. The times are simulated.
256 devices in a mesh: dp: 32 (over y, z_lo, core), seq: 8 (over z_hi, x).
Axes of the slice: x: 4, y: 4, z: 8 (z_hi: 2, z_lo: 4; z = z_hi * 4 + z_lo), core: 2. Of those that a mesh axis runs over, the one named last changes fastest.
Arguments:
- query: bfloat16 [36864, 2048], P(('dp', 'seq')), may hold values from -32 to 32
- key_in: bfloat16 [36864, 2048], P(('dp', 'seq')), may hold values from -6.5 to 6.5
- value: bfloat16 [36864, 2048], P(('dp', 'seq')), may hold values from -6 to 6
- out_weight: bfloat16 [2048, 3072], P('dp'), may hold values from -0.125 to 0.125
- out_grad: bfloat16 [36864, 3072], P(('dp', 'seq')), may hold values from -6 to 6
- windows: int32 [96, 5], P('dp'), may hold values from 0 to 95, as said below
- window_count: int32 [96], P('dp'), may hold values from 1 to 5, as said below
Outputs:
- output: bfloat16 [36864, 3072], P(('dp', 'seq'))
- d_query: bfloat16 [36864, 2048], P(('dp', 'seq'))
- d_key: bfloat16 [36864, 2048], P(('dp', 'seq'))
- d_value: bfloat16 [36864, 2048], P(('dp', 'seq'))
Inputs may be any that keep to these rules, and one draw needn't show every extreme that they name: `windows`: row t names 5 different tiles; its first entry is t itself, and every entry lies in tile t's slab or in the slab just before or after it, a slab being 3 consecutive tiles. Tile t attends to the first window_count[t] tiles of its row; some tile attends to all 5 and some to one.
All inputs are finite; a program needn't handle non-finite values.
Results may differ from a plain program's by a relative error of at most 0.0075.
Values may be sent and summed in bfloat16 or wider, within the bound.
A program may use at most 192 MiB of HBM per device.

v0:
```python
import jax
import jax.numpy as jnp
from jax import lax
from jax.sharding import PartitionSpec as P

HD = 128
TILE = 384


def extended_2(block, sides, width):
    for axis, dim in sides:
        count = lax.axis_size(axis)
        forward = [(i, i + 1) for i in range(count - 1)]
        backward = [(target, source) for source, target in forward]
        low = lax.ppermute(
            lax.slice_in_dim(block, block.shape[dim] - width, None, axis=dim), axis, forward
        )
        high = lax.ppermute(lax.slice_in_dim(block, 0, width, axis=dim), axis, backward)
        block = jnp.concatenate([low, block, high], axis=dim)
    return block


def make_fold(source, out_grad, portion):
    out_sum = jnp.dot(source, portion, preferred_element_type=jnp.float32)
    product = jnp.einsum("td,rd->tr", out_grad, portion, preferred_element_type=jnp.float32).astype(
        jnp.bfloat16
    )
    return (out_sum, product)


def body(query, key_in, value, out_weight, out_grad, windows, window_count):
    tile_count = windows.shape[0]
    window = windows.shape[1]
    factor = HD ** (-0.5)
    q_heads, k_heads, v_heads = (
        lax.all_to_all(query, "seq", split_axis=1, concat_axis=0, tiled=True),
        lax.all_to_all(key_in, "seq", split_axis=1, concat_axis=0, tiled=True),
        lax.all_to_all(value, "seq", split_axis=1, concat_axis=0, tiled=True),
    )
    slab_rows = q_heads.shape[0]
    width_local = q_heads.shape[1]
    head_count = width_local // HD
    stacked = jnp.concatenate([k_heads, v_heads], axis=1)
    extended = extended_2(stacked, (("dp", 0),), slab_rows)
    blocks = extended.reshape(3 * tile_count, TILE, 2, head_count, HD)
    lowest = (lax.axis_index("dp") - 1) * tile_count
    local_ids = windows - lowest
    query_tiles = q_heads.reshape(tile_count, TILE, head_count, HD)

    def forward_tile(members):
        query_tile, tile_ids, filled = members
        gathered = blocks[tile_ids]
        keyed_rows = gathered[:, :, 0]
        value_rows = gathered[:, :, 1]
        scores = (
            jnp.einsum("qhd,wkhd->hqwk", query_tile, keyed_rows, preferred_element_type=jnp.float32)
            * factor
        )
        allowed = (jnp.arange(window) < filled)[None, None, :, None]
        scores = jnp.where(allowed, scores, -jnp.inf)
        largest = jnp.max(scores, axis=(2, 3), keepdims=True)
        raised = jnp.exp(scores - largest)
        total = jnp.sum(raised, axis=(2, 3), keepdims=True)
        weights = raised / total
        attn_tile = jnp.einsum(
            "hqwk,wkhd->qhd",
            weights.astype(jnp.bfloat16),
            value_rows,
            preferred_element_type=jnp.float32,
        ).astype(jnp.bfloat16)
        return (attn_tile, weights, largest[:, :, 0, 0], total[:, :, 0, 0])

    attn_tiles, saved_weights, saved_largest, saved_total = lax.map(
        forward_tile, (query_tiles, local_ids, window_count)
    )
    attn_heads = attn_tiles.reshape(slab_rows, width_local)
    attn_tokens = lax.all_to_all(attn_heads, "seq", split_axis=0, concat_axis=1, tiled=True)
    out_sum, grad_tokens = make_fold(
        attn_tokens, out_grad, lax.all_gather(out_weight, "dp", axis=0, tiled=True)
    )
    output = out_sum.astype(jnp.bfloat16)
    grad_heads = lax.all_to_all(grad_tokens, "seq", split_axis=1, concat_axis=0, tiled=True)
    grad_tiles = grad_heads.reshape(tile_count, TILE, head_count, HD)

    def backward_tile(members):
        query_tile, tile_ids, weights, grad_tile = members
        gathered = blocks[tile_ids]
        keyed_rows = gathered[:, :, 0]
        value_rows = gathered[:, :, 1]
        rounded = weights.astype(jnp.bfloat16)
        grad_weights = jnp.einsum(
            "qhd,wkhd->hqwk", grad_tile, value_rows, preferred_element_type=jnp.float32
        )
        centre = jnp.sum(weights * grad_weights, axis=(2, 3), keepdims=True)
        grad_scores = (weights * (grad_weights - centre) * factor).astype(jnp.bfloat16)
        grad_query = jnp.einsum(
            "hqwk,wkhd->qhd", grad_scores, keyed_rows, preferred_element_type=jnp.float32
        ).astype(jnp.bfloat16)
        grad_keyed = jnp.einsum(
            "hqwk,qhd->wkhd", grad_scores, query_tile, preferred_element_type=jnp.float32
        )
        grad_valued = jnp.einsum(
            "hqwk,qhd->wkhd", rounded, grad_tile, preferred_element_type=jnp.float32
        )
        return (grad_query, grad_keyed, grad_valued, centre[:, :, 0, 0])

    query_grads, keyed_parts, valued_parts, saved_centre = lax.map(
        backward_tile, (query_tiles, local_ids, saved_weights, grad_tiles)
    )
    flat_size = TILE * width_local
    onehot = (local_ids.reshape(-1)[:, None] == jnp.arange(3 * tile_count)[None, :]).astype(
        jnp.float32
    )
    keyed_ext = jnp.einsum(
        "ns,nx->sx",
        onehot,
        keyed_parts.reshape(tile_count * window, flat_size),
        precision=lax.Precision.HIGHEST,
    ).reshape(3 * slab_rows, width_local)
    valued_ext = jnp.einsum(
        "ns,nx->sx",
        onehot,
        valued_parts.reshape(tile_count * window, flat_size),
        precision=lax.Precision.HIGHEST,
    ).reshape(3 * slab_rows, width_local)
    combined = jnp.concatenate([keyed_ext, valued_ext], axis=1)
    outer_rims = jnp.concatenate([combined[:slab_rows], combined[2 * slab_rows :]], axis=0)
    arrived = extended_2(outer_rims.astype(jnp.bfloat16), (("dp", 0),), slab_rows).astype(
        outer_rims.dtype
    )
    summed = combined[slab_rows : 2 * slab_rows] + arrived[:slab_rows] + arrived[3 * slab_rows :]
    key_heads = summed[:, :width_local].astype(jnp.bfloat16)
    value_heads = summed[:, width_local:].astype(jnp.bfloat16)
    query_heads = query_grads.reshape(slab_rows, width_local)
    d_query, d_key, d_value = (
        lax.all_to_all(query_heads, "seq", split_axis=0, concat_axis=1, tiled=True),
        lax.all_to_all(key_heads, "seq", split_axis=0, concat_axis=1, tiled=True),
        lax.all_to_all(value_heads, "seq", split_axis=0, concat_axis=1, tiled=True),
    )
    return (output, d_query, d_key, d_value)


def solution(mesh):
    in_specs = (
        P(("dp", "seq"), None),
        P(("dp", "seq"), None),
        P(("dp", "seq"), None),
        P("dp", None),
        P(("dp", "seq"), None),
        P("dp", None),
        P("dp"),
    )
    out_specs = (
        P(("dp", "seq"), None),
        P(("dp", "seq"), None),
        P(("dp", "seq"), None),
        P(("dp", "seq"), None),
    )
    return jax.shard_map(body, mesh=mesh, in_specs=in_specs, out_specs=out_specs, check_vma=False)
```

profile of v0, /device:TPU:32, one launch (start us, length us, event | category | flops | bytes accessed | tf_op | source)
XLA Modules:
  0.0 524.1 jit_solution(6442156912303026273)
XLA Ops:
  9.9 10.0 %all-to-all-start.1 = ((bf16[144,8,256]{2,0,1:T(8,128)(2,1)}), bf16[144,8,256]{2,0,1:T(8,128)(2,1)S(1)}, u32[]{:S(2)}, u32[]{:S(2)}) async-start(bf16[144,8,256]{2,0,1:T(8,128)(2,1)} %bitcast.149), calls=%async_computation.1 | async-start | bytes 1179648 | tf_op jit(solution)/shard_map/all_to_all | solution.py:38
  21.0 24.1 %all-to-all-done.1 = bf16[144,8,256]{2,0,1:T(8,128)(2,1)S(1)} async-done(((bf16[144,8,256]{2,0,1:T(8,128)(2,1)}), bf16[144,8,256]{2,0,1:T(8,128)(2,1)S(1)}, u32[]{:S(2)}, u32[]{:S(2)}) %all-to-all-start.1) | async-done | bytes 589856 | tf_op jit(solution)/shard_map/all_to_all | solution.py:38
  45.1 28.5 %all_to_all.146 = bf16[144,8,256]{2,0,1:T(8,128)(2,1)S(1)} all-to-all(bf16[144,8,256]{2,0,1:T(8,128)(2,1)S(1)} %bitcast.210), channel_id=1, replica_groups=mesh['dp'=32,'seq'=8] {'seq'}, dimensions={1} | all-to-all | bytes 1179648 | tf_op jit(solution)/shard_map/all_to_all | solution.py:37
  79.9 3.5 all-to-all-start.2
  84.1 64.2 %all-to-all-done.2 = bf16[144,8,256]{2,0,1:T(8,128)(2,1)S(1)} async-done(((bf16[144,8,256]{2,0,1:T(8,128)(2,1)}), bf16[144,8,256]{2,0,1:T(8,128)(2,1)S(1)}, u32[]{:S(2)}, u32[]{:S(2)}) %all-to-all-start.2) | async-done | bytes 589856 | tf_op jit(solution)/shard_map/all_to_all | solution.py:36
  148.4 3.6 pad_maximum_fusion
  152.0 8.4 %reshape.123 = bf16[9,384,2,2,128]{4,3,2,1,0:T(2,128)(2,1)} reshape(bf16[3456,512]{1,0:T(8,128)(2,1)} %pad_maximum_fusion) | data formatting | bytes 7077888 | tf_op jit(solution)/shard_map/reshape | solution.py:45
  160.4 4.6 copy.130
  164.9 8.9 %convolution_convert_fusion.1 = bf16[144,2048]{1,0:T(8,128)(2,1)S(1)} fusion(bf16[144,3072]{1,0:T(8,128)(2,1)S(1)} %copy-done, bf16[2048,3072]{1,0:T(8,128)(2,1)} %all-gather.2.cloned.1.call-done), kind=kOutput, calls=%fused_computation.55 | convolution fusion | flops 1812234240 | bytes 14057472 | tf_op jit(solution)/shard_map/td,rd->tr/dot_general | solution.py:25
  174.7 8.0 %all-to-all-start.4 = ((bf16[144,8,256]{2,0,1:T(8,128)(2,1)}), bf16[144,8,256]{2,0,1:T(8,128)(2,1)}, u32[]{:S(2)}, u32[]{:S(2)}) async-start(bf16[144,8,256]{2,0,1:T(8,128)(2,1)} %bitcast.147), calls=%async_computation.4 | async-start | bytes 1179648 | tf_op jit(solution)/shard_map/all_to_all | solution.py:82
  183.8 64.0 %while.26 = (s32[]{:T(128)}, bf16[3,384,2,128]{3,2,1,0:T(2,128)(2,1)}, f32[3,2,384,5,384]{2,4,3,1,0:T(8,128)}, s32[3,5]{1,0:T(4,128)S(1)}, bf16[9,384,2,2,128]{4...) while((s32[]{:T(128)}, bf16[3,384,2,128]{3,2,1,0:T(2,128)(2,1)}, ...), condition=%wide.region_3.4_spmd, body=%wide.region_0.3_spmd.sunk | while | flops 778665472 | bytes 66479360 | solution.py:73
  183.8 2.9 gather_fusion
  198.7 6.5 %bitcast_dynamic-update-slice_fusion.2 = f32[3,2,384,5,384]{2,4,3,1,0:T(8,128)} fusion(f32[3,2,384,5,384]{2,4,3,1,0:T(8,128)} %get-tuple-element.357, s32[]{:T(128)S(6)} %copy.236, f32[2,384]{1,0:T(2,128)S(1)} %fusion.72, f32[2,384]{1,0:T(2,128)S(1)} %get-tuple-element.331, f32[2,384,5,384]{1,3,2,0:T(8,128)} %copy-done.2, ...), kind=kLoop, calls=%fused_computation.2.clone.1 | loop fusion | flops 5898240 | bytes 11802633 | tf_op jit(solution)/shard_map/while/body/jit(dynamic_update_index_in_dim)/dynamic_update_slice | solution.py:73
  220.1 6.4 %bitcast_dynamic-update-slice_fusion.2 = f32[3,2,384,5,384]{2,4,3,1,0:T(8,128)} fusion(f32[3,2,384,5,384]{2,4,3,1,0:T(8,128)} %get-tuple-element.357, s32[]{:T(128)S(6)} %copy.236, f32[2,384]{1,0:T(2,128)S(1)} %fusion.72, f32[2,384]{1,0:T(2,128)S(1)} %get-tuple-element.331, f32[2,384,5,384]{1,3,2,0:T(8,128)} %copy-done.2, ...), kind=kLoop, calls=%fused_computation.2.clone.1 | loop fusion | flops 5898240 | bytes 11802633 | tf_op jit(solution)/shard_map/while/body/jit(dynamic_update_index_in_dim)/dynamic_update_slice | solution.py:73
  241.4 6.4 %bitcast_dynamic-update-slice_fusion.2 = f32[3,2,384,5,384]{2,4,3,1,0:T(8,128)} fusion(f32[3,2,384,5,384]{2,4,3,1,0:T(8,128)} %get-tuple-element.357, s32[]{:T(128)S(6)} %copy.236, f32[2,384]{1,0:T(2,128)S(1)} %fusion.72, f32[2,384]{1,0:T(2,128)S(1)} %get-tuple-element.331, f32[2,384,5,384]{1,3,2,0:T(8,128)} %copy-done.2, ...), kind=kLoop, calls=%fused_computation.2.clone.1 | loop fusion | flops 5898240 | bytes 11802633 | tf_op jit(solution)/shard_map/while/body/jit(dynamic_update_index_in_dim)/dynamic_update_slice | solution.py:73
  250.7 104.2 %while.27 = (s32[]{:T(128)}, bf16[3,384,2,128]{3,2,1,0:T(2,128)(2,1)}, f32[3,5,384,2,128]{4,3,2,1,0:T(2,128)}, f32[3,5,384,2,128]{4,3,2,1,0:T(2,128)}, s32[3,5]{...) while((s32[]{:T(128)}, ...), condition=%wide.region_6.7_spmd, body=%wide.region_4.6_spmd.sunk | while | flops 1518895360 | bytes 78260528 | solution.py:107
  250.9 3.1 gather_fusion.1
  255.3 3.7 fusion.80
  259.0 5.4 %fusion.81 = bf16[2,384,5,384]{1,3,2,0:T(8,128)(2,1)} fusion(f32[2,384,5,384]{1,3,2,0:T(8,128)S(1)} %get-tuple-element.342, f32[3,2,384,5,384]{2,4,3,1,0:T(8,128)} %get-tuple-element.397, s32[]{:T(128)S(6)} %copy.246, f32[2,384]{1,0:T(2,128)S(1)} %get-tuple-element.343), kind=kLoop, calls=%fused_computation.30.clone.1 | loop fusion | flops 5898240 | bytes 14748676 | tf_op jit(solution)/shard_map/while/body/eval_jaxpr/convert_element_type | solution.py:95
  268.6 3.7 fusion.83
  281.2 4.3 constant_dynamic-update-slice_fusion.11
  285.6 3.1 gather_fusion.1
  289.9 3.7 fusion.80
  293.6 5.4 %fusion.81 = bf16[2,384,5,384]{1,3,2,0:T(8,128)(2,1)} fusion(f32[2,384,5,384]{1,3,2,0:T(8,128)S(1)} %get-tuple-element.342, f32[3,2,384,5,384]{2,4,3,1,0:T(8,128)} %get-tuple-element.397, s32[]{:T(128)S(6)} %copy.246, f32[2,384]{1,0:T(2,128)S(1)} %get-tuple-element.343), kind=kLoop, calls=%fused_computation.30.clone.1 | loop fusion | flops 5898240 | bytes 14748676 | tf_op jit(solution)/shard_map/while/body/eval_jaxpr/convert_element_type | solution.py:95
  303.2 3.7 fusion.83
  315.9 4.4 constant_dynamic-update-slice_fusion.11
  320.3 3.1 gather_fusion.1
  324.6 3.7 fusion.80
  328.3 5.4 %fusion.81 = bf16[2,384,5,384]{1,3,2,0:T(8,128)(2,1)} fusion(f32[2,384,5,384]{1,3,2,0:T(8,128)S(1)} %get-tuple-element.342, f32[3,2,384,5,384]{2,4,3,1,0:T(8,128)} %get-tuple-element.397, s32[]{:T(128)S(6)} %copy.246, f32[2,384]{1,0:T(2,128)S(1)} %get-tuple-element.343), kind=kLoop, calls=%fused_computation.30.clone.1 | loop fusion | flops 5898240 | bytes 14748676 | tf_op jit(solution)/shard_map/while/body/eval_jaxpr/convert_element_type | solution.py:95
  337.9 3.7 fusion.83
  350.6 4.3 constant_dynamic-update-slice_fusion.11
  354.9 8.6 %reshape.126 = f32[15,98304]{1,0:T(8,128)} reshape(f32[3,5,384,2,128]{4,3,2,1,0:T(2,128)} %get-tuple-element.94) | data formatting | bytes 11796480 | tf_op jit(solution)/shard_map/reshape | solution.py:117
  363.5 8.1 %fusion.35 = f32[9,98304]{1,0:T(8,128)} fusion(f32[15,98304]{1,0:T(8,128)} %reshape.126, s32[15]{0:T(128)S(1)} %copy-done.8), kind=kOutput, calls=%fused_computation.69 | convolution fusion | flops 159252608 | bytes 9437244 | tf_op jit(solution)/shard_map/ns,nx->sx/dot_general | solution.py:114
  371.6 4.3 reshape.127
  375.9 4.2 constant_dynamic-update-slice_fusion.5
  380.1 8.5 %reshape.128 = f32[15,98304]{1,0:T(8,128)} reshape(f32[3,5,384,2,128]{4,3,2,1,0:T(2,128)} %get-tuple-element.95) | data formatting | bytes 11796480 | tf_op jit(solution)/shard_map/reshape | solution.py:123
  388.6 8.1 %fusion.34 = f32[9,98304]{1,0:T(8,128)} fusion(f32[15,98304]{1,0:T(8,128)} %reshape.128, s32[15]{0:T(128)S(1)} %copy-done.8), kind=kOutput, calls=%fused_computation.68 | convolution fusion | flops 159252608 | bytes 9437244 | tf_op jit(solution)/shard_map/ns,nx->sx/dot_general | solution.py:120
  396.7 4.1 reshape.129
  400.8 4.1 constant_dynamic-update-slice_fusion.4
  404.9 3.5 convert.10
  414.1 9.6 %all-to-all-start.3 = ((bf16[8,144,256]{2,1,0:T(8,128)(2,1)}), bf16[8,144,256]{2,1,0:T(8,128)(2,1)S(1)}, u32[]{:S(2)}, u32[]{:S(2)}) async-start(bf16[8,144,256]{2,1,0:T(8,128)(2,1)} %all_to_all.119), calls=%async_computation.3 | async-start | bytes 1179648 | tf_op jit(solution)/shard_map/all_to_all | solution.py:77
  426.5 32.6 %all-to-all-done.3 = bf16[8,144,256]{2,1,0:T(8,128)(2,1)S(1)} async-done(((bf16[8,144,256]{2,1,0:T(8,128)(2,1)}), bf16[8,144,256]{2,1,0:T(8,128)(2,1)S(1)}, u32[]{:S(2)}, u32[]{:S(2)}) %all-to-all-start.3) | async-done | bytes 589856 | tf_op jit(solution)/shard_map/all_to_all | solution.py:77
  459.1 4.2 all-to-all-start.5
  463.4 6.8 %fusion.33 = bf16[1152,512]{1,0:T(8,128)(2,1)S(1)} fusion(f32[3456,512]{1,0:T(8,128)} %constant_dynamic-update-slice_fusion.4, bf16[1152,512]{1,0:T(8,128)(2,1)} %collective-permute-done.3, bf16[1152,512]{1,0:T(8,128)(2,1)S(1)} %get-tuple-element.225, bf16[1152,512]{1,0:T(8,128)(2,1)S(1)} %get-tuple-element.226, bf16[1152,512]{1,0:T(8,128)(2,1)} %collective-permute-done.2), kind=kLoop, calls=%fused_computation.58 | loop fusion | flops 11206656 | bytes 8257536 | tf_op jit(solution)/shard_map/convert.1
  471.0 8.0 %all-to-all-done.5 = bf16[8,144,256]{2,1,0:T(8,128)(2,1)} async-done(((bf16[8,144,256]{2,1,0:T(8,128)(2,1)}), bf16[8,144,256]{2,1,0:T(8,128)(2,1)}, u32[]{:S(2)}, u32[]{:S(2)}) %all-to-all-start.5) | async-done | bytes 589856 | tf_op jit(solution)/shard_map/all_to_all | solution.py:136
  479.0 21.2 %all_to_all.147 = bf16[8,144,256]{2,1,0:T(8,128)(2,1)S(1)} all-to-all(bf16[8,144,256]{2,1,0:T(8,128)(2,1)S(1)} %bitcast.211), channel_id=1, replica_groups=mesh['dp'=32,'seq'=8] {'seq'}, dimensions={0} | all-to-all | bytes 1179648 | tf_op jit(solution)/shard_map/all_to_all | solution.py:137
  500.2 3.5 all-to-all-start.7
  503.8 7.6 %convolution_convert_fusion = bf16[144,3072]{1,0:T(8,128)(2,1)} fusion(bf16[144,2048]{1,0:T(8,128)(2,1)S(1)} %bitcast.205, bf16[2048,3072]{1,0:T(8,128)(2,1)} %all-gather.2.cloned.1.call-done), kind=kOutput, calls=%fused_computation.53 | convolution fusion | flops 1812381696 | bytes 14057472 | tf_op jit(solution)/shard_map/dot_general | solution.py:24
  (150 shorter events, 115.2 us)
Async XLA Ops:
  7.2 157.8 %copy-start = (bf16[144,3072]{1,0:T(8,128)(2,1)S(1)}, bf16[144,3072]{1,0:T(8,128)(2,1)}, u32[]{:S(2)}) copy-start(bf16[144,3072]{1,0:T(8,128)(2,1)} %param.15) | copy-start | bytes 2654212
  7.2 71.8 %copy-start.7 = (bf16[144,2048]{1,0:T(8,128)(2,1)S(1)}, bf16[144,2048]{1,0:T(8,128)(2,1)}, u32[]{:S(2)}) copy-start(bf16[144,2048]{1,0:T(8,128)(2,1)} %param.11) | copy-start | bytes 1769476
  7.2 76.3 %copy-start.9 = (s32[3,5]{1,0:T(4,128)S(1)}, s32[3,5]{1,0:T(4,128)}, u32[]{:S(2)}) copy-start(s32[3,5]{1,0:T(4,128)} %param.16) | copy-start | bytes 184
  7.2 157.7 %all-gather.2.cloned.1.call-start = ((), (), s32[]{:S(2)}) async-start(), calls=%async_computation.8 | async-start | bytes 12976128 | tf_op jit(solution)/shard_map/all_gather | solution.py:79
  9.9 35.2 %all-to-all-start.1 = ((bf16[144,8,256]{2,0,1:T(8,128)(2,1)}), bf16[144,8,256]{2,0,1:T(8,128)(2,1)S(1)}, u32[]{:S(2)}, u32[]{:S(2)}) async-start(bf16[144,8,256]{2,0,1:T(8,128)(2,1)} %bitcast.149), calls=%async_computation.1 | async-start | bytes 1179648 | tf_op jit(solution)/shard_map/all_to_all | solution.py:38
  74.7 73.8 %collective-permute-start.1 = (bf16[1152,512]{1,0:T(8,128)(2,1)}, bf16[1152,512]{1,0:T(8,128)(2,1)}, u32[]{:S(2)}, u32[]{:S(2)}) collective-permute-start(bf16[1152,512]{1,0:T(8,128)(2,1)} %pad_maximum_fusion.4), channel_id=1, source_target_pairs={{8,0},{16,8},{24,16},{32,24},{40,32},{48,40},{56,48},{64,56},{72,6... | collective-permute-start | bytes 3538952 | tf_op jit(solution)/shard_map/ppermute | solution.py:18
  76.6 71.9 %collective-permute-start = (bf16[1152,512]{1,0:T(8,128)(2,1)}, bf16[1152,512]{1,0:T(8,128)(2,1)}, u32[]{:S(2)}, u32[]{:S(2)}) collective-permute-start(bf16[1152,512]{1,0:T(8,128)(2,1)} %pad_maximum_fusion.4), channel_id=1, source_target_pairs={{0,8},{8,16},{16,24},{24,32},{32,40},{40,48},{48,56},{56,64},{64,7... | collective-permute-start | bytes 3538952 | tf_op jit(solution)/shard_map/ppermute | solution.py:15
  79.9 68.4 %all-to-all-start.2 = ((bf16[144,8,256]{2,0,1:T(8,128)(2,1)}), bf16[144,8,256]{2,0,1:T(8,128)(2,1)S(1)}, u32[]{:S(2)}, u32[]{:S(2)}) async-start(bf16[144,8,256]{2,0,1:T(8,128)(2,1)} %bitcast.148), calls=%async_computation.2 | async-start | bytes 1179648 | tf_op jit(solution)/shard_map/all_to_all | solution.py:36
  164.9 18.8 %copy-start.10 = (s32[3]{0:T(128)S(1)}, s32[3]{0:T(128)}, u32[]{:S(2)}) copy-start(s32[3]{0:T(128)} %param.17) | copy-start | bytes 40
  174.7 73.1 %all-to-all-start.4 = ((bf16[144,8,256]{2,0,1:T(8,128)(2,1)}), bf16[144,8,256]{2,0,1:T(8,128)(2,1)}, u32[]{:S(2)}, u32[]{:S(2)}) async-start(bf16[144,8,256]{2,0,1:T(8,128)(2,1)} %bitcast.147), calls=%async_computation.4 | async-start | bytes 1179648 | tf_op jit(solution)/shard_map/all_to_all | solution.py:82
  193.4 2.5 copy-start.2
  214.9 2.5 copy-start.2
  236.1 2.5 copy-start.2
  250.9 8.1 %copy-start.4 = (bf16[3,384,2,128]{3,2,1,0:T(2,128)(2,1)}, bf16[3,384,2,128]{3,2,1,0:T(2,128)(2,1)S(1)}, u32[]{:S(2)}) copy-start(bf16[3,384,2,128]{3,2,1,0:T(2,128)(2,1)S(1)} %get-tuple-element.398) | copy-start | bytes 1769476 | tf_op jit(solution)/shard_map/while
  259.0 5.4 %copy-start.3 = (bf16[5,384,1,2,128]{4,1,3,2,0:T(8,128)(2,1)S(1)}, bf16[5,384,1,2,128]{4,1,3,2,0:T(8,128)(2,1)}, u32[]{:S(2)}) copy-start(bf16[5,384,1,2,128]{4,1,3,2,0:T(8,128)(2,1)} %get-tuple-element.344) | copy-start | bytes 2949124 | tf_op jit(solution)/shard_map/while
  278.3 7.2 %copy-start.5 = (bf16[3,384,2,128]{3,2,1,0:T(2,128)(2,1)S(1)}, bf16[3,384,2,128]{3,2,1,0:T(2,128)(2,1)}, u32[]{:S(2)}) copy-start(bf16[3,384,2,128]{3,2,1,0:T(2,128)(2,1)} %copy-done.4) | copy-start | bytes 1769476 | tf_op jit(solution)/shard_map/while
  285.5 8.1 %copy-start.4 = (bf16[3,384,2,128]{3,2,1,0:T(2,128)(2,1)}, bf16[3,384,2,128]{3,2,1,0:T(2,128)(2,1)S(1)}, u32[]{:S(2)}) copy-start(bf16[3,384,2,128]{3,2,1,0:T(2,128)(2,1)S(1)} %get-tuple-element.398) | copy-start | bytes 1769476 | tf_op jit(solution)/shard_map/while
  293.6 5.4 %copy-start.3 = (bf16[5,384,1,2,128]{4,1,3,2,0:T(8,128)(2,1)S(1)}, bf16[5,384,1,2,128]{4,1,3,2,0:T(8,128)(2,1)}, u32[]{:S(2)}) copy-start(bf16[5,384,1,2,128]{4,1,3,2,0:T(8,128)(2,1)} %get-tuple-element.344) | copy-start | bytes 2949124 | tf_op jit(solution)/shard_map/while
  313.0 7.3 %copy-start.5 = (bf16[3,384,2,128]{3,2,1,0:T(2,128)(2,1)S(1)}, bf16[3,384,2,128]{3,2,1,0:T(2,128)(2,1)}, u32[]{:S(2)}) copy-start(bf16[3,384,2,128]{3,2,1,0:T(2,128)(2,1)} %copy-done.4) | copy-start | bytes 1769476 | tf_op jit(solution)/shard_map/while
  320.2 8.1 %copy-start.4 = (bf16[3,384,2,128]{3,2,1,0:T(2,128)(2,1)}, bf16[3,384,2,128]{3,2,1,0:T(2,128)(2,1)S(1)}, u32[]{:S(2)}) copy-start(bf16[3,384,2,128]{3,2,1,0:T(2,128)(2,1)S(1)} %get-tuple-element.398) | copy-start | bytes 1769476 | tf_op jit(solution)/shard_map/while
  328.3 5.4 %copy-start.3 = (bf16[5,384,1,2,128]{4,1,3,2,0:T(8,128)(2,1)S(1)}, bf16[5,384,1,2,128]{4,1,3,2,0:T(8,128)(2,1)}, u32[]{:S(2)}) copy-start(bf16[5,384,1,2,128]{4,1,3,2,0:T(8,128)(2,1)} %get-tuple-element.344) | copy-start | bytes 2949124 | tf_op jit(solution)/shard_map/while
  347.6 7.3 %copy-start.5 = (bf16[3,384,2,128]{3,2,1,0:T(2,128)(2,1)S(1)}, bf16[3,384,2,128]{3,2,1,0:T(2,128)(2,1)}, u32[]{:S(2)}) copy-start(bf16[3,384,2,128]{3,2,1,0:T(2,128)(2,1)} %copy-done.4) | copy-start | bytes 1769476 | tf_op jit(solution)/shard_map/while
  354.9 8.6 %copy-start.8 = (s32[15]{0:T(128)S(1)}, s32[15]{0:T(128)}, u32[]{:S(2)}) copy-start(s32[15]{0:T(128)} %eq.15) | copy-start | bytes 184
  404.9 8.0 %copy-start.6 = (bf16[3,384,2,128]{3,2,1,0:T(2,128)(2,1)S(1)}, bf16[3,384,2,128]{3,2,1,0:T(2,128)(2,1)}, u32[]{:S(2)}) copy-start(bf16[3,384,2,128]{3,2,1,0:T(2,128)(2,1)} %get-tuple-element.91) | copy-start | bytes 1769476
  408.6 54.8 %collective-permute-start.3 = (bf16[1152,512]{1,0:T(8,128)(2,1)S(1)}, bf16[1152,512]{1,0:T(8,128)(2,1)}, u32[]{:S(2)}, u32[]{:S(2)}) collective-permute-start(bf16[1152,512]{1,0:T(8,128)(2,1)S(1)} %get-tuple-element.226), channel_id=1, source_target_pairs={{8,0},{16,8},{24,16},{32,24},{40,32},{48,40},{56,48},{64,56},{72,6... | collective-permute-start | bytes 3538952 | tf_op jit(solution)/shard_map/ppermute | solution.py:18
  410.5 52.8 %collective-permute-start.2 = (bf16[1152,512]{1,0:T(8,128)(2,1)S(1)}, bf16[1152,512]{1,0:T(8,128)(2,1)}, u32[]{:S(2)}, u32[]{:S(2)}) collective-permute-start(bf16[1152,512]{1,0:T(8,128)(2,1)S(1)} %get-tuple-element.225), channel_id=1, source_target_pairs={{0,8},{8,16},{16,24},{24,32},{32,40},{40,48},{48,56},{56,64},{64,7... | collective-permute-start | bytes 3538952 | tf_op jit(solution)/shard_map/ppermute | solution.py:15
  414.1 45.0 %all-to-all-start.3 = ((bf16[8,144,256]{2,1,0:T(8,128)(2,1)}), bf16[8,144,256]{2,1,0:T(8,128)(2,1)S(1)}, u32[]{:S(2)}, u32[]{:S(2)}) async-start(bf16[8,144,256]{2,1,0:T(8,128)(2,1)} %all_to_all.119), calls=%async_computation.3 | async-start | bytes 1179648 | tf_op jit(solution)/shard_map/all_to_all | solution.py:77
  459.1 19.9 %all-to-all-start.5 = ((bf16[8,144,256]{2,1,0:T(8,128)(2,1)}), bf16[8,144,256]{2,1,0:T(8,128)(2,1)}, u32[]{:S(2)}, u32[]{:S(2)}) async-start(bf16[8,144,256]{2,1,0:T(8,128)(2,1)} %all_to_all.126), calls=%async_computation.5 | async-start | bytes 1179648 | tf_op jit(solution)/shard_map/all_to_all | solution.py:136
  500.2 15.9 %all-to-all-start.7 = ((bf16[8,144,256]{2,1,0:T(8,128)(2,1)}), bf16[8,144,256]{2,1,0:T(8,128)(2,1)S(1)}, u32[]{:S(2)}, u32[]{:S(2)}) async-start(bf16[8,144,256]{2,1,0:T(8,128)(2,1)} %bitcast.43), calls=%async_computation.7 | async-start | bytes 1179648 | tf_op jit(solution)/shard_map/all_to_all | solution.py:138
  503.8 13.2 %copy-start.1 = (bf16[144,3072]{1,0:T(8,128)(2,1)S(1)}, bf16[144,3072]{1,0:T(8,128)(2,1)}, u32[]{:S(2)}) copy-start(bf16[144,3072]{1,0:T(8,128)(2,1)} %param.15) | copy-start | bytes 2654212
Sparse Core Ops, SparseCore 0:
  9.9 140.2 all-gather.1
where the time goes:
time: 532 us; the launch traced here: 524 us
  local copies, waits for them, and re-layouts  141 us (27%)
  waiting for transfers between devices  132 us (25%)
  matrix products  82.6 us (16%)
  other arithmetic  56.4 us (11%)
  blocking collectives  49.7 us (9%)
  starting transfers between devices  47.6 us (9%)
  between operations  14.5 us (3%)
    all_to_all x1, waiting for transfers between devices, body(): lax.all_to_all(query, 'seq', split_axis=1, concat_axis=0, tiled=True)  64.2 us
    all_to_all x1, waiting for transfers between devices, body(): lax.all_to_all(attn_heads, 'seq', split_axis=0, concat_axis=1, tiled=True)  32.6 us
    dynamic_update_slice x9, local copies, waits for them, and re-layouts, body(): lax.map(backward_tile, (query_tiles, local_ids, saved_weights, grad_tiles))  30.4 us
    all_to_all x1, blocking collectives, body(): lax.all_to_all(key_in, 'seq', split_axis=1, concat_axis=0, tiled=True)  28.5 us
    all_to_all x1, waiting for transfers between devices, body(): lax.all_to_all(value, 'seq', split_axis=1, concat_axis=0, tiled=True)  24.1 us
    all_to_all x1, blocking collectives, body(): lax.all_to_all(key_heads, 'seq', split_axis=0, concat_axis=1, tiled=True)  21.2 us
    dynamic_update_slice x3, other arithmetic, body(): lax.map(forward_tile, (query_tiles, local_ids, window_count))  19.3 us
    convert_element_type x3, other arithmetic, backward_tile(): (weights * (grad_weights - centre) * factor).astype(jnp.bfloat16)  16.2 us
  transfers between devices with their start and end apart: 11, of which 5 were waited for; matrix products, arithmetic and copies ran while one was open for 19% of the time, Pallas kernels for 0%

commit v1 on v0

--- a/solution.py
+++ b/solution.py
@@ -35,7 +35,10 @@
     q_heads, k_heads, v_heads = (
         lax.all_to_all(query, "seq", split_axis=1, concat_axis=0, tiled=True),
         lax.all_to_all(key_in, "seq", split_axis=1, concat_axis=0, tiled=True),
-        lax.all_to_all(value, "seq", split_axis=1, concat_axis=0, tiled=True),
+        jnp.concatenate(
+            lax.all_to_all(jnp.stack(jnp.split(value, lax.axis_size("seq"), axis=1)), "seq", 0, 0),
+            axis=0,
+        ),
     )
     slab_rows = q_heads.shape[0]
     width_local = q_heads.shape[1]

time: 532 us -> 531 us (level)
  local copies, waits for them, and re-layouts: 141 us -> 151 us
  waiting for transfers between devices: 132 us -> 124 us
    unnamed x15 -> x22, local copies, waits for them, and re-layouts: 4.21 us -> 14.9 us
  transfers between devices with their start and end apart: 11 -> 11, of which waited for: 5 -> 5; matrix products, arithmetic and copies ran while one was open for 19% -> 21% of each run, Pallas kernels for 0% -> 0%
where the time goes in v1:
time: 531 us; the launch traced here: 523 us
  local copies, waits for them, and re-layouts  151 us (28%)
  waiting for transfers between devices  124 us (23%)
  matrix products  82.6 us (16%)
  other arithmetic  56.4 us (11%)
  blocking collectives  48.9 us (9%)
  starting transfers between devices  44.2 us (8%)
  between operations  14.5 us (3%)
    all_to_all x1, waiting for transfers between devices, body(): lax.all_to_all(query, 'seq', split_axis=1, concat_axis=0, tiled=True)  59.5 us
    all_to_all x1, blocking collectives, body(): lax.all_to_all(key_in, 'seq', split_axis=1, concat_axis=0, tiled=True)  31.4 us
    all_to_all x1, waiting for transfers between devices, body(): lax.all_to_all(attn_heads, 'seq', split_axis=0, concat_axis=1, tiled=True)  31.1 us
    dynamic_update_slice x9, local copies, waits for them, and re-layouts, body(): lax.map(backward_tile, (query_tiles, local_ids, saved_weights, grad_tiles))  30.4 us
    all_to_all x1, waiting for transfers between devices, body(): lax.all_to_all(jnp.stack(jnp.split(value, lax.axis_size('seq'), axis=1)),...  24.8 us
    dynamic_update_slice x3, other arithmetic, body(): lax.map(forward_tile, (query_tiles, local_ids, window_count))  19.3 us
    all_to_all x1, blocking collectives, body(): lax.all_to_all(key_heads, 'seq', split_axis=0, concat_axis=1, tiled=True)  17.5 us
    convert_element_type x3, other arithmetic, backward_tile(): (weights * (grad_weights - centre) * factor).astype(jnp.bfloat16)  16.2 us
  transfers between devices with their start and end apart: 11, of which 5 were waited for; matrix products, arithmetic and copies ran while one was open for 21% of the time, Pallas kernels for 0%

profile of v1, /device:TPU:32, one launch (start us, length us, event | category | flops | bytes accessed | tf_op | source)
XLA Modules:
  0.0 522.7 jit_solution(4604646354567845550)
XLA Ops:
  20.1 10.0 %all-to-all-start.1 = ((bf16[8,144,256]{2,1,0:T(8,128)(2,1)}), bf16[8,144,256]{2,1,0:T(8,128)(2,1)S(1)}, u32[]{:S(2)}, u32[]{:S(2)}) async-start(bf16[8,144,256]{2,1,0:T(8,128)(2,1)} %bitcast_dynamic-update-slice_fusion.1), calls=%async_computation.1 | async-start | bytes 1179648 | tf_op jit(solution)/shard_map/all_to_all | solution.py:39
  31.3 24.8 %all-to-all-done.1 = bf16[8,144,256]{2,1,0:T(8,128)(2,1)S(1)} async-done(((bf16[8,144,256]{2,1,0:T(8,128)(2,1)}), bf16[8,144,256]{2,1,0:T(8,128)(2,1)S(1)}, u32[]{:S(2)}, u32[]{:S(2)}) %all-to-all-start.1) | async-done | bytes 589856 | tf_op jit(solution)/shard_map/all_to_all | solution.py:39
  56.1 31.4 %all_to_all.132 = bf16[144,8,256]{2,0,1:T(8,128)(2,1)S(1)} all-to-all(bf16[144,8,256]{2,0,1:T(8,128)(2,1)S(1)} %bitcast.220), channel_id=1, replica_groups=mesh['dp'=32,'seq'=8] {'seq'}, dimensions={1} | all-to-all | bytes 1179648 | tf_op jit(solution)/shard_map/all_to_all | solution.py:37
  93.8 3.5 all-to-all-start.2
  98.0 59.5 %all-to-all-done.2 = bf16[144,8,256]{2,0,1:T(8,128)(2,1)S(1)} async-done(((bf16[144,8,256]{2,0,1:T(8,128)(2,1)}), bf16[144,8,256]{2,0,1:T(8,128)(2,1)S(1)}, u32[]{:S(2)}, u32[]{:S(2)}) %all-to-all-start.2) | async-done | bytes 589856 | tf_op jit(solution)/shard_map/all_to_all | solution.py:36
  157.6 3.5 pad_maximum_fusion
  161.2 8.4 %reshape.124 = bf16[9,384,2,2,128]{4,3,2,1,0:T(2,128)(2,1)} reshape(bf16[3456,512]{1,0:T(8,128)(2,1)} %pad_maximum_fusion) | data formatting | bytes 7077888 | tf_op jit(solution)/shard_map/reshape | solution.py:48
  169.5 4.6 copy.102
  174.1 8.9 %convolution_convert_fusion.1 = bf16[144,2048]{1,0:T(8,128)(2,1)S(1)} fusion(bf16[144,3072]{1,0:T(8,128)(2,1)S(1)} %copy-done, bf16[2048,3072]{1,0:T(8,128)(2,1)} %all-gather.2.cloned.1.call-done), kind=kOutput, calls=%fused_computation.55 | convolution fusion | flops 1812234240 | bytes 14057472 | tf_op jit(solution)/shard_map/td,rd->tr/dot_general | solution.py:25
  183.8 4.7 all-to-all-start.4
  189.6 64.0 %while.26 = (s32[]{:T(128)}, bf16[3,384,2,128]{3,2,1,0:T(2,128)(2,1)}, f32[3,2,384,5,384]{2,4,3,1,0:T(8,128)}, s32[3,5]{1,0:T(4,128)S(1)}, bf16[9,384,2,2,128]{4...) while((s32[]{:T(128)}, bf16[3,384,2,128]{3,2,1,0:T(2,128)(2,1)}, ...), condition=%wide.region_3.4_spmd, body=%wide.region_0.3_spmd.sunk | while | flops 778665472 | bytes 66479360 | solution.py:76
  204.5 6.5 %bitcast_dynamic-update-slice_fusion.10 = f32[3,2,384,5,384]{2,4,3,1,0:T(8,128)} fusion(f32[3,2,384,5,384]{2,4,3,1,0:T(8,128)} %get-tuple-element.341, s32[]{:T(128)S(6)} %copy.212, f32[2,384]{1,0:T(2,128)S(1)} %fusion.72, f32[2,384]{1,0:T(2,128)S(1)} %get-tuple-element.315, f32[2,384,5,384]{1,3,2,0:T(8,128)} %copy-done.2, ...), kind=kLoop, calls=%fused_computation.2.clone.1 | loop fusion | flops 5898240 | bytes 11802633 | tf_op jit(solution)/shard_map/while/body/jit(dynamic_update_index_in_dim)/dynamic_update_slice | solution.py:76
  225.9 6.4 %bitcast_dynamic-update-slice_fusion.10 = f32[3,2,384,5,384]{2,4,3,1,0:T(8,128)} fusion(f32[3,2,384,5,384]{2,4,3,1,0:T(8,128)} %get-tuple-element.341, s32[]{:T(128)S(6)} %copy.212, f32[2,384]{1,0:T(2,128)S(1)} %fusion.72, f32[2,384]{1,0:T(2,128)S(1)} %get-tuple-element.315, f32[2,384,5,384]{1,3,2,0:T(8,128)} %copy-done.2, ...), kind=kLoop, calls=%fused_computation.2.clone.1 | loop fusion | flops 5898240 | bytes 11802633 | tf_op jit(solution)/shard_map/while/body/jit(dynamic_update_index_in_dim)/dynamic_update_slice | solution.py:76
  247.2 6.4 %bitcast_dynamic-update-slice_fusion.10 = f32[3,2,384,5,384]{2,4,3,1,0:T(8,128)} fusion(f32[3,2,384,5,384]{2,4,3,1,0:T(8,128)} %get-tuple-element.341, s32[]{:T(128)S(6)} %copy.212, f32[2,384]{1,0:T(2,128)S(1)} %fusion.72, f32[2,384]{1,0:T(2,128)S(1)} %get-tuple-element.315, f32[2,384,5,384]{1,3,2,0:T(8,128)} %copy-done.2, ...), kind=kLoop, calls=%fused_computation.2.clone.1 | loop fusion | flops 5898240 | bytes 11802633 | tf_op jit(solution)/shard_map/while/body/jit(dynamic_update_index_in_dim)/dynamic_update_slice | solution.py:76
  256.6 104.2 %while.27 = (s32[]{:T(128)}, bf16[3,384,2,128]{3,2,1,0:T(2,128)(2,1)}, f32[3,5,384,2,128]{4,3,2,1,0:T(2,128)}, f32[3,5,384,2,128]{4,3,2,1,0:T(2,128)}, s32[3,5]{...) while((s32[]{:T(128)}, ...), condition=%wide.region_6.7_spmd, body=%wide.region_4.6_spmd.sunk | while | flops 1518895360 | bytes 78260528 | solution.py:110
  256.8 3.1 gather_fusion.1
  261.1 3.7 fusion.80
  264.8 5.4 %fusion.81 = bf16[2,384,5,384]{1,3,2,0:T(8,128)(2,1)} fusion(f32[2,384,5,384]{1,3,2,0:T(8,128)S(1)} %get-tuple-element.326, f32[3,2,384,5,384]{2,4,3,1,0:T(8,128)} %get-tuple-element.381, s32[]{:T(128)S(6)} %copy.222, f32[2,384]{1,0:T(2,128)S(1)} %get-tuple-element.327), kind=kLoop, calls=%fused_computation.30.clone.1 | loop fusion | flops 5898240 | bytes 14748676 | tf_op jit(solution)/shard_map/while/body/eval_jaxpr/convert_element_type | solution.py:98
  274.4 3.7 fusion.83
  287.1 4.3 constant_dynamic-update-slice_fusion.11
  291.4 3.1 gather_fusion.1
  295.8 3.7 fusion.80
  299.5 5.4 %fusion.81 = bf16[2,384,5,384]{1,3,2,0:T(8,128)(2,1)} fusion(f32[2,384,5,384]{1,3,2,0:T(8,128)S(1)} %get-tuple-element.326, f32[3,2,384,5,384]{2,4,3,1,0:T(8,128)} %get-tuple-element.381, s32[]{:T(128)S(6)} %copy.222, f32[2,384]{1,0:T(2,128)S(1)} %get-tuple-element.327), kind=kLoop, calls=%fused_computation.30.clone.1 | loop fusion | flops 5898240 | bytes 14748676 | tf_op jit(solution)/shard_map/while/body/eval_jaxpr/convert_element_type | solution.py:98
  309.1 3.7 fusion.83
  321.7 4.4 constant_dynamic-update-slice_fusion.11
  326.1 3.1 gather_fusion.1
  330.5 3.7 fusion.80
  334.2 5.4 %fusion.81 = bf16[2,384,5,384]{1,3,2,0:T(8,128)(2,1)} fusion(f32[2,384,5,384]{1,3,2,0:T(8,128)S(1)} %get-tuple-element.326, f32[3,2,384,5,384]{2,4,3,1,0:T(8,128)} %get-tuple-element.381, s32[]{:T(128)S(6)} %copy.222, f32[2,384]{1,0:T(2,128)S(1)} %get-tuple-element.327), kind=kLoop, calls=%fused_computation.30.clone.1 | loop fusion | flops 5898240 | bytes 14748676 | tf_op jit(solution)/shard_map/while/body/eval_jaxpr/convert_element_type | solution.py:98
  343.8 3.7 fusion.83
  356.4 4.3 constant_dynamic-update-slice_fusion.11
  360.8 8.6 %reshape.127 = f32[15,98304]{1,0:T(8,128)} reshape(f32[3,5,384,2,128]{4,3,2,1,0:T(2,128)} %get-tuple-element.94) | data formatting | bytes 11796480 | tf_op jit(solution)/shard_map/reshape | solution.py:120
  369.3 8.1 %fusion.35 = f32[9,98304]{1,0:T(8,128)} fusion(f32[15,98304]{1,0:T(8,128)} %reshape.127, s32[15]{0:T(128)S(1)} %copy-done.8), kind=kOutput, calls=%fused_computation.78 | convolution fusion | flops 159252608 | bytes 9437244 | tf_op jit(solution)/shard_map/ns,nx->sx/dot_general | solution.py:117
  377.5 4.3 reshape.128
  381.8 4.2 constant_dynamic-update-slice_fusion.5
  386.0 8.5 %reshape.129 = f32[15,98304]{1,0:T(8,128)} reshape(f32[3,5,384,2,128]{4,3,2,1,0:T(2,128)} %get-tuple-element.95) | data formatting | bytes 11796480 | tf_op jit(solution)/shard_map/reshape | solution.py:126
  394.4 8.1 %fusion.34 = f32[9,98304]{1,0:T(8,128)} fusion(f32[15,98304]{1,0:T(8,128)} %reshape.129, s32[15]{0:T(128)S(1)} %copy-done.8), kind=kOutput, calls=%fused_computation.77 | convolution fusion | flops 159252608 | bytes 9437244 | tf_op jit(solution)/shard_map/ns,nx->sx/dot_general | solution.py:123
  402.6 4.1 reshape.130
  406.7 4.1 constant_dynamic-update-slice_fusion.4
  410.8 3.5 convert.10
  420.0 9.6 %all-to-all-start.3 = ((bf16[8,144,256]{2,1,0:T(8,128)(2,1)}), bf16[8,144,256]{2,1,0:T(8,128)(2,1)S(1)}, u32[]{:S(2)}, u32[]{:S(2)}) async-start(bf16[8,144,256]{2,1,0:T(8,128)(2,1)} %all_to_all.105), calls=%async_computation.3 | async-start | bytes 1179648 | tf_op jit(solution)/shard_map/all_to_all | solution.py:80
  432.3 31.1 %all-to-all-done.3 = bf16[8,144,256]{2,1,0:T(8,128)(2,1)S(1)} async-done(((bf16[8,144,256]{2,1,0:T(8,128)(2,1)}), bf16[8,144,256]{2,1,0:T(8,128)(2,1)S(1)}, u32[]{:S(2)}, u32[]{:S(2)}) %all-to-all-start.3) | async-done | bytes 589856 | tf_op jit(solution)/shard_map/all_to_all | solution.py:80
  463.4 4.2 all-to-all-start.5
  467.6 6.8 %fusion.33 = bf16[1152,512]{1,0:T(8,128)(2,1)S(1)} fusion(f32[3456,512]{1,0:T(8,128)} %constant_dynamic-update-slice_fusion.4, bf16[1152,512]{1,0:T(8,128)(2,1)} %collective-permute-done.3, bf16[1152,512]{1,0:T(8,128)(2,1)S(1)} %get-tuple-element.209, bf16[1152,512]{1,0:T(8,128)(2,1)S(1)} %get-tuple-element.210, bf16[1152,512]{1,0:T(8,128)(2,1)} %collective-permute-done.2), kind=kLoop, calls=%fused_computation.58 | loop fusion | flops 11206656 | bytes 8257536 | tf_op jit(solution)/shard_map/convert.1
  475.3 4.9 all-to-all-done.5
  480.2 17.5 %all_to_all.133 = bf16[8,144,256]{2,1,0:T(8,128)(2,1)S(1)} all-to-all(bf16[8,144,256]{2,1,0:T(8,128)(2,1)S(1)} %bitcast.221), channel_id=1, replica_groups=mesh['dp'=32,'seq'=8] {'seq'}, dimensions={0} | all-to-all | bytes 1179648 | tf_op jit(solution)/shard_map/all_to_all | solution.py:140
  497.7 3.5 all-to-all-start.7
  501.3 7.6 %convolution_convert_fusion = bf16[144,3072]{1,0:T(8,128)(2,1)} fusion(bf16[144,2048]{1,0:T(8,128)(2,1)S(1)} %bitcast.215, bf16[2048,3072]{1,0:T(8,128)(2,1)} %all-gather.2.cloned.1.call-done), kind=kOutput, calls=%fused_computation.53 | convolution fusion | flops 1812381696 | bytes 14057472 | tf_op jit(solution)/shard_map/dot_general | solution.py:24
  511.7 3.0 all-to-all-done.7
  (157 shorter events, 126.5 us)
Async XLA Ops:
  7.2 166.9 %copy-start = (bf16[144,3072]{1,0:T(8,128)(2,1)S(1)}, bf16[144,3072]{1,0:T(8,128)(2,1)}, u32[]{:S(2)}) copy-start(bf16[144,3072]{1,0:T(8,128)(2,1)} %param.15) | copy-start | bytes 2654212
  7.2 85.8 %copy-start.7 = (bf16[144,2048]{1,0:T(8,128)(2,1)S(1)}, bf16[144,2048]{1,0:T(8,128)(2,1)}, u32[]{:S(2)}) copy-start(bf16[144,2048]{1,0:T(8,128)(2,1)} %param.11) | copy-start | bytes 1769476
  7.2 90.2 %copy-start.9 = (s32[3,5]{1,0:T(4,128)S(1)}, s32[3,5]{1,0:T(4,128)}, u32[]{:S(2)}) copy-start(s32[3,5]{1,0:T(4,128)} %param.16) | copy-start | bytes 184
  7.2 166.9 %all-gather.2.cloned.1.call-start = ((), (), s32[]{:S(2)}) async-start(), calls=%async_computation.8 | async-start | bytes 12976128 | tf_op jit(solution)/shard_map/all_gather | solution.py:82
  20.1 36.0 %all-to-all-start.1 = ((bf16[8,144,256]{2,1,0:T(8,128)(2,1)}), bf16[8,144,256]{2,1,0:T(8,128)(2,1)S(1)}, u32[]{:S(2)}, u32[]{:S(2)}) async-start(bf16[8,144,256]{2,1,0:T(8,128)(2,1)} %bitcast_dynamic-update-slice_fusion.1), calls=%async_computation.1 | async-start | bytes 1179648 | tf_op jit(solution)/shard_map/all_to_all | solution.py:39
  88.6 69.0 %collective-permute-start.1 = (bf16[1152,512]{1,0:T(8,128)(2,1)}, bf16[1152,512]{1,0:T(8,128)(2,1)}, u32[]{:S(2)}, u32[]{:S(2)}) collective-permute-start(bf16[1152,512]{1,0:T(8,128)(2,1)} %pad_maximum_fusion.4), channel_id=1, source_target_pairs={{8,0},{16,8},{24,16},{32,24},{40,32},{48,40},{56,48},{64,56},{72,6... | collective-permute-start | bytes 3538952 | tf_op jit(solution)/shard_map/ppermute | solution.py:18
  90.5 67.1 %collective-permute-start = (bf16[1152,512]{1,0:T(8,128)(2,1)}, bf16[1152,512]{1,0:T(8,128)(2,1)}, u32[]{:S(2)}, u32[]{:S(2)}) collective-permute-start(bf16[1152,512]{1,0:T(8,128)(2,1)} %pad_maximum_fusion.4), channel_id=1, source_target_pairs={{0,8},{8,16},{16,24},{24,32},{32,40},{40,48},{48,56},{56,64},{64,7... | collective-permute-start | bytes 3538952 | tf_op jit(solution)/shard_map/ppermute | solution.py:15
  93.8 63.7 %all-to-all-start.2 = ((bf16[144,8,256]{2,0,1:T(8,128)(2,1)}), bf16[144,8,256]{2,0,1:T(8,128)(2,1)S(1)}, u32[]{:S(2)}, u32[]{:S(2)}) async-start(bf16[144,8,256]{2,0,1:T(8,128)(2,1)} %bitcast.159), calls=%async_computation.2 | async-start | bytes 1179648 | tf_op jit(solution)/shard_map/all_to_all | solution.py:36
  174.1 15.5 %copy-start.10 = (s32[3]{0:T(128)S(1)}, s32[3]{0:T(128)}, u32[]{:S(2)}) copy-start(s32[3]{0:T(128)} %param.17) | copy-start | bytes 40
  183.8 69.8 %all-to-all-start.4 = ((bf16[144,8,256]{2,0,1:T(8,128)(2,1)}), bf16[144,8,256]{2,0,1:T(8,128)(2,1)}, u32[]{:S(2)}, u32[]{:S(2)}) async-start(bf16[144,8,256]{2,0,1:T(8,128)(2,1)} %bitcast.158), calls=%async_computation.4 | async-start | bytes 1179648 | tf_op jit(solution)/shard_map/all_to_all | solution.py:85
  199.3 2.5 copy-start.2
  220.7 2.5 copy-start.2
  242.0 2.5 copy-start.2
  256.7 8.1 %copy-start.4 = (bf16[3,384,2,128]{3,2,1,0:T(2,128)(2,1)}, bf16[3,384,2,128]{3,2,1,0:T(2,128)(2,1)S(1)}, u32[]{:S(2)}) copy-start(bf16[3,384,2,128]{3,2,1,0:T(2,128)(2,1)S(1)} %get-tuple-element.382) | copy-start | bytes 1769476 | tf_op jit(solution)/shard_map/while
  264.8 5.4 %copy-start.3 = (bf16[5,384,1,2,128]{4,1,3,2,0:T(8,128)(2,1)S(1)}, bf16[5,384,1,2,128]{4,1,3,2,0:T(8,128)(2,1)}, u32[]{:S(2)}) copy-start(bf16[5,384,1,2,128]{4,1,3,2,0:T(8,128)(2,1)} %get-tuple-element.328) | copy-start | bytes 2949124 | tf_op jit(solution)/shard_map/while
  284.2 7.2 %copy-start.5 = (bf16[3,384,2,128]{3,2,1,0:T(2,128)(2,1)S(1)}, bf16[3,384,2,128]{3,2,1,0:T(2,128)(2,1)}, u32[]{:S(2)}) copy-start(bf16[3,384,2,128]{3,2,1,0:T(2,128)(2,1)} %copy-done.4) | copy-start | bytes 1769476 | tf_op jit(solution)/shard_map/while
  291.4 8.1 %copy-start.4 = (bf16[3,384,2,128]{3,2,1,0:T(2,128)(2,1)}, bf16[3,384,2,128]{3,2,1,0:T(2,128)(2,1)S(1)}, u32[]{:S(2)}) copy-start(bf16[3,384,2,128]{3,2,1,0:T(2,128)(2,1)S(1)} %get-tuple-element.382) | copy-start | bytes 1769476 | tf_op jit(solution)/shard_map/while
  299.5 5.4 %copy-start.3 = (bf16[5,384,1,2,128]{4,1,3,2,0:T(8,128)(2,1)S(1)}, bf16[5,384,1,2,128]{4,1,3,2,0:T(8,128)(2,1)}, u32[]{:S(2)}) copy-start(bf16[5,384,1,2,128]{4,1,3,2,0:T(8,128)(2,1)} %get-tuple-element.328) | copy-start | bytes 2949124 | tf_op jit(solution)/shard_map/while
  318.8 7.3 %copy-start.5 = (bf16[3,384,2,128]{3,2,1,0:T(2,128)(2,1)S(1)}, bf16[3,384,2,128]{3,2,1,0:T(2,128)(2,1)}, u32[]{:S(2)}) copy-start(bf16[3,384,2,128]{3,2,1,0:T(2,128)(2,1)} %copy-done.4) | copy-start | bytes 1769476 | tf_op jit(solution)/shard_map/while
  326.1 8.1 %copy-start.4 = (bf16[3,384,2,128]{3,2,1,0:T(2,128)(2,1)}, bf16[3,384,2,128]{3,2,1,0:T(2,128)(2,1)S(1)}, u32[]{:S(2)}) copy-start(bf16[3,384,2,128]{3,2,1,0:T(2,128)(2,1)S(1)} %get-tuple-element.382) | copy-start | bytes 1769476 | tf_op jit(solution)/shard_map/while
  334.2 5.4 %copy-start.3 = (bf16[5,384,1,2,128]{4,1,3,2,0:T(8,128)(2,1)S(1)}, bf16[5,384,1,2,128]{4,1,3,2,0:T(8,128)(2,1)}, u32[]{:S(2)}) copy-start(bf16[5,384,1,2,128]{4,1,3,2,0:T(8,128)(2,1)} %get-tuple-element.328) | copy-start | bytes 2949124 | tf_op jit(solution)/shard_map/while
  353.5 7.3 %copy-start.5 = (bf16[3,384,2,128]{3,2,1,0:T(2,128)(2,1)S(1)}, bf16[3,384,2,128]{3,2,1,0:T(2,128)(2,1)}, u32[]{:S(2)}) copy-start(bf16[3,384,2,128]{3,2,1,0:T(2,128)(2,1)} %copy-done.4) | copy-start | bytes 1769476 | tf_op jit(solution)/shard_map/while
  360.8 8.6 %copy-start.8 = (s32[15]{0:T(128)S(1)}, s32[15]{0:T(128)}, u32[]{:S(2)}) copy-start(s32[15]{0:T(128)} %eq.15) | copy-start | bytes 184
  410.8 8.0 %copy-start.6 = (bf16[3,384,2,128]{3,2,1,0:T(2,128)(2,1)S(1)}, bf16[3,384,2,128]{3,2,1,0:T(2,128)(2,1)}, u32[]{:S(2)}) copy-start(bf16[3,384,2,128]{3,2,1,0:T(2,128)(2,1)} %get-tuple-element.91) | copy-start | bytes 1769476
  414.5 53.2 %collective-permute-start.3 = (bf16[1152,512]{1,0:T(8,128)(2,1)S(1)}, bf16[1152,512]{1,0:T(8,128)(2,1)}, u32[]{:S(2)}, u32[]{:S(2)}) collective-permute-start(bf16[1152,512]{1,0:T(8,128)(2,1)S(1)} %get-tuple-element.210), channel_id=1, source_target_pairs={{8,0},{16,8},{24,16},{32,24},{40,32},{48,40},{56,48},{64,56},{72,6... | collective-permute-start | bytes 3538952 | tf_op jit(solution)/shard_map/ppermute | solution.py:18
  416.4 51.3 %collective-permute-start.2 = (bf16[1152,512]{1,0:T(8,128)(2,1)S(1)}, bf16[1152,512]{1,0:T(8,128)(2,1)}, u32[]{:S(2)}, u32[]{:S(2)}) collective-permute-start(bf16[1152,512]{1,0:T(8,128)(2,1)S(1)} %get-tuple-element.209), channel_id=1, source_target_pairs={{0,8},{8,16},{16,24},{24,32},{32,40},{40,48},{48,56},{56,64},{64,7... | collective-permute-start | bytes 3538952 | tf_op jit(solution)/shard_map/ppermute | solution.py:15
  420.0 43.4 %all-to-all-start.3 = ((bf16[8,144,256]{2,1,0:T(8,128)(2,1)}), bf16[8,144,256]{2,1,0:T(8,128)(2,1)S(1)}, u32[]{:S(2)}, u32[]{:S(2)}) async-start(bf16[8,144,256]{2,1,0:T(8,128)(2,1)} %all_to_all.105), calls=%async_computation.3 | async-start | bytes 1179648 | tf_op jit(solution)/shard_map/all_to_all | solution.py:80
  463.4 16.8 %all-to-all-start.5 = ((bf16[8,144,256]{2,1,0:T(8,128)(2,1)}), bf16[8,144,256]{2,1,0:T(8,128)(2,1)}, u32[]{:S(2)}, u32[]{:S(2)}) async-start(bf16[8,144,256]{2,1,0:T(8,128)(2,1)} %all_to_all.112), calls=%async_computation.5 | async-start | bytes 1179648 | tf_op jit(solution)/shard_map/all_to_all | solution.py:139
  497.7 17.1 %all-to-all-start.7 = ((bf16[8,144,256]{2,1,0:T(8,128)(2,1)}), bf16[8,144,256]{2,1,0:T(8,128)(2,1)S(1)}, u32[]{:S(2)}, u32[]{:S(2)}) async-start(bf16[8,144,256]{2,1,0:T(8,128)(2,1)} %bitcast.50), calls=%async_computation.7 | async-start | bytes 1179648 | tf_op jit(solution)/shard_map/all_to_all | solution.py:141
  501.3 14.3 %copy-start.1 = (bf16[144,3072]{1,0:T(8,128)(2,1)S(1)}, bf16[144,3072]{1,0:T(8,128)(2,1)}, u32[]{:S(2)}) copy-start(bf16[144,3072]{1,0:T(8,128)(2,1)} %param.15) | copy-start | bytes 2654212
Sparse Core Ops, SparseCore 0:
  9.9 132.3 all-gather.1
